TPU v7x, 32 devices: a whole 2x2x4 slice. The times are simulated.
32 devices in a mesh: dp: 4 (over y, x), fsdp: 8 (over z, core).
Axes of the slice: x: 2, y: 2, z: 4, core: 2. Of those that a mesh axis runs over, the one named last changes fastest.
Arguments:
- tokens: bfloat16 [12288, 8192], P(('dp', 'fsdp')), may hold values from -6 to 6
- frozen_value_weight: bfloat16 [8192, 1024], P('fsdp'), may hold values from -0.0625 to 0.0625
- adapter_down_weight: bfloat16 [32, 8192, 64], P('dp', 'fsdp'), may hold values from -0.0625 to 0.0625
- adapter_up_weight: bfloat16 [32, 64, 1024], P('dp', None, 'fsdp'), may hold values from -0.75 to 0.75
- output_gradient: bfloat16 [12288, 1024], P(('dp', 'fsdp')), may hold values from -6 to 6
- adapter_per_block: int32 [96], P(('dp', 'fsdp')), may hold values from 0 to 31, as said below
- block_live_count: int32 [96], P(('dp', 'fsdp')), may hold values from 1 to 128
Outputs:
- values: bfloat16 [12288, 1024], P(('dp', 'fsdp'))
- input_gradient: bfloat16 [12288, 8192], P(('dp', 'fsdp'))
- grad_down: float32 [32, 8192, 64], P('dp', 'fsdp')
- grad_up: float32 [32, 64, 1024], P('dp', None, 'fsdp')
Inputs may be any that keep to these rules, and one draw needn't show every extreme that they name: `adapter_per_block`: within the blocks of one device the adapter numbers never fall.
All inputs are finite; a program needn't handle non-finite values.
Results may differ from a plain program's by a relative error of at most 0.0038.
Values may be sent and summed in bfloat16 or wider, within the bound.
A program may use at most 192 MiB of HBM per device.

v0:
```python
import jax
import jax.numpy as jnp
from jax import lax
from jax.sharding import PartitionSpec as P

adapter_scale = 0.5


def body(
    tokens,
    frozen_value_weight,
    adapter_down_weight,
    adapter_up_weight,
    output_gradient,
    adapter_per_block,
    block_live_count,
):
    count_dev = tokens.shape[0]
    per_dev = adapter_per_block.shape[0]
    block_rows = count_dev // per_dev
    adapter_list = adapter_down_weight.shape[0] * lax.axis_size("dp")
    piece = lax.all_gather(frozen_value_weight, "fsdp", axis=0, tiled=True)
    forward_pass = jnp.dot(tokens, piece, preferred_element_type=jnp.float32)
    portion_gradient = lax.dot_general(
        output_gradient, piece, (((1,), (1,)), ((), ())), preferred_element_type=jnp.float32
    )
    down_all, up_all = (
        lax.all_gather(adapter_down_weight, "dp", axis=0, tiled=True),
        lax.all_gather(adapter_up_weight, "dp", axis=0, tiled=True),
    )
    ids_all, fill_all = (
        lax.all_gather(adapter_per_block, "fsdp", axis=0, tiled=True),
        lax.all_gather(block_live_count, "fsdp", axis=0, tiled=True),
    )
    positions = jnp.arange(block_rows, dtype=jnp.int32)
    catalog = jnp.arange(adapter_list, dtype=jnp.int32)
    live_slot_mask = (positions[None, :] < fill_all[:, None]).astype(jnp.float32)[:, :, None]
    choose = (ids_all[:, None] == catalog[None, :]).astype(jnp.float32)
    down_per_block = down_all[ids_all]
    group_blocks = ids_all.shape[0]
    group_rows = group_blocks * block_rows
    x_group, dy_group = (
        lax.all_to_all(tokens, "fsdp", split_axis=1, concat_axis=0, tiled=True),
        lax.all_to_all(output_gradient, "fsdp", split_axis=1, concat_axis=0, tiled=True),
    )
    input_per_block = x_group.reshape(group_blocks, block_rows, -1)
    dy_blocks = dy_group.reshape(group_blocks, block_rows, -1)
    up_per_block = up_all[ids_all]
    down_partial = jnp.einsum(
        "gzq,gqx->gzx", input_per_block, down_per_block, preferred_element_type=jnp.float32
    )
    up_partial = jnp.einsum(
        "bkc,brc->bkr", dy_blocks, up_per_block, preferred_element_type=jnp.float32
    )
    down_total, up_total = lax.psum((down_partial, up_partial), "fsdp")
    reduced_down_output = (down_total * live_slot_mask).astype(jnp.bfloat16)
    reduced_output_gradient = (up_total * live_slot_mask).astype(jnp.bfloat16)
    raised_rows = (
        jnp.einsum(
            "bkr,brc->bkc", reduced_down_output, up_per_block, preferred_element_type=jnp.float32
        )
        .astype(jnp.bfloat16)
        .reshape(group_rows, -1)
    )
    spread_input = (
        jnp.einsum(
            "qjz,qaz->qja",
            reduced_output_gradient,
            down_per_block,
            preferred_element_type=jnp.float32,
        )
        .astype(jnp.bfloat16)
        .reshape(group_rows, -1)
    )
    raised_resident, input_resident = (
        lax.all_to_all(raised_rows, "fsdp", split_axis=0, concat_axis=1, tiled=True),
        lax.all_to_all(spread_input, "fsdp", split_axis=0, concat_axis=1, tiled=True),
    )
    up_terms = jnp.einsum(
        "bkr,bkc->brc", reduced_down_output, dy_blocks, preferred_element_type=jnp.float32
    )
    up_gradient = jnp.einsum("ba,brc->arc", choose, up_terms, precision=lax.Precision.HIGHEST)
    down_gradient_terms = jnp.einsum(
        "uia,uiw->uaw", input_per_block, reduced_output_gradient, preferred_element_type=jnp.float32
    )
    down_gradient = jnp.einsum(
        "ba,bdr->adr", choose, down_gradient_terms, precision=lax.Precision.HIGHEST
    )
    grad_down, grad_up = (
        lax.psum_scatter(adapter_scale * down_gradient, "dp", scatter_dimension=0, tiled=True),
        lax.psum_scatter(adapter_scale * up_gradient, "dp", scatter_dimension=0, tiled=True),
    )
    values = (forward_pass + adapter_scale * raised_resident.astype(jnp.float32)).astype(
        jnp.bfloat16
    )
    input_gradient = (portion_gradient + adapter_scale * input_resident.astype(jnp.float32)).astype(
        jnp.bfloat16
    )
    return (values, input_gradient, grad_down, grad_up)


def solution(mesh):
    placed = (
        P(("dp", "fsdp"), None),
        P("fsdp", None),
        P("dp", "fsdp", None),
        P("dp", None, "fsdp"),
        P(("dp", "fsdp"), None),
        P(("dp", "fsdp")),
        P(("dp", "fsdp")),
    )
    return jax.shard_map(
        body,
        mesh=mesh,
        in_specs=placed,
        out_specs=(
            P(("dp", "fsdp"), None),
            P(("dp", "fsdp"), None),
            P("dp", "fsdp", None),
            P("dp", None, "fsdp"),
        ),
        check_vma=False,
    )
```

profile of v0, /device:TPU:0, one launch (start us, length us, event | category | flops | bytes accessed | tf_op | source)
XLA Modules:
  0.0 620.4 jit_solution(18002532766082441934)
XLA Ops:
  7.2 0.0 copy-start
  7.2 1.1 copy-done
  8.3 1.0 copy_bitcast_fusion.1
  9.3 6.4 %all-to-all-start.2 = ((bf16[384,8,128]{2,0,1:T(8,128)(2,1)}), bf16[384,8,128]{2,0,1:T(8,128)(2,1)S(1)}, u32[]{:S(2)}, u32[]{:S(2)}) async-start(bf16[384,8,128]{2,0,1:T(8,128)(2,1)} %copy_bitcast_fusion.1), calls=%async_computation.2 | async-start | bytes 1572864 | tf_op jit(solution)/shard_map/all_to_all | solution.py:44
  15.7 6.5 %copy.40 = bf16[48,8,8,1024]{3,2,0,1:T(8,128)(2,1)} copy(bf16[48,8,8,1024]{3,2,1,0:T(8,128)(2,1)} %bitcast.60) | data formatting | bytes 12582912 | tf_op jit(solution)/shard_map/all_to_all | solution.py:43
  22.2 14.4 %all-to-all-done.2 = bf16[384,8,128]{2,0,1:T(8,128)(2,1)S(1)} async-done(((bf16[384,8,128]{2,0,1:T(8,128)(2,1)}), bf16[384,8,128]{2,0,1:T(8,128)(2,1)S(1)}, u32[]{:S(2)}, u32[]{:S(2)}) %all-to-all-start.2) | async-done | bytes 786464 | tf_op jit(solution)/shard_map/all_to_all | solution.py:44
  36.6 0.0 copy-start.7
  36.6 0.0 copy-start.5
  36.6 0.0 copy-start.6
  36.6 0.0 copy-start.4
  36.6 4.9 all-to-all-start
  41.5 0.0 all-gather.5.cloned.1.call-start
  41.6 0.7 all-gather.5.cloned.1.call-update
  42.3 0.0 all-reduce.6.cloned.1.call-start
  42.3 0.0 copy-done.7
  42.3 0.6 dynamic-slice
  43.6 0.0 copy-done.5
  43.6 0.2 dynamic-update-slice
  43.8 0.0 copy-done.6
  43.8 0.2 dynamic-update-slice.1
  44.1 136.5 %all-reduce.2 = (s32[24]{0:T(128)S(1)}, s32[24]{0:T(128)S(1)}) all-reduce(s32[24]{0:T(128)S(1)} %dynamic-update-slice, s32[24]{0:T(128)S(1)} %dynamic-update-slice.1), channel_id=1, replica_groups=mesh['dp'=4,'fsdp'=8] {'fsdp'}, use_global_device_ids=true, to_apply=%add | all-reduce | flops 48 | bytes 384
  180.6 0.0 copy-done.4
  180.6 10.0 %all_gather.19 = bf16[32,64,128]{2,1,0:T(8,128)(2,1)S(1)} all-gather(bf16[8,64,128]{2,1,0:T(8,128)(2,1)S(1)} %copy-done.4), channel_id=1, replica_groups=mesh['dp'=4,'fsdp'=8] {'dp'}, dimensions={0}, use_global_device_ids=true | all-gather | bytes 655360 | tf_op jit(solution)/shard_map/all_gather | solution.py:29
  190.7 0.6 gather_fusion.1
  191.3 1.5 convolution_bitcast_fusion
  192.8 0.0 all-gather.5.cloned.1.call-done
  192.8 4.7 gather_fusion
  197.5 0.0 all-to-all-done
  197.5 6.9 %convolution_bitcast_fusion.1 = f32[24,128,64]{1,2,0:T(8,128)} fusion(bf16[24,1024,64]{1,2,0:T(8,128)(2,1)} %gather_fusion, bf16[24,128,1024]{2,1,0:T(8,128)(2,1)} %bitcast.2), kind=kOutput, calls=%fused_computation.16 | convolution fusion | flops 402653184 | bytes 10223616 | tf_op jit(solution)/shard_map/gzq,gqx->gzx/dot_general | solution.py:49
  204.4 0.0 all-reduce.6.cloned.1.call-update
  204.4 0.0 reduce-scatter.5.cloned.1.call-start
  204.5 0.1 fusion.9
  204.5 60.0 %all-reduce.6.cloned.1.call-done = (f32[24,128,64]{1,2,0:T(8,128)}, f32[24,128,64]{1,2,0:T(8,128)}) async-done(((f32[24,128,64]{1,2,0:T(8,128)}, f32[24,128,64]{1,2,0:T(8,128)}), (f32[24,128,64]{1,2,0:T(8,128)}, f32[24,128,64]{1,2,0:T(8,128)})) %all-reduce.6.cloned.1.call-update) | async-done | bytes 1572880 | tf_op jit(solution)/shard_map/psum | solution.py:55
  264.6 1.5 fusion.7
  266.0 2.1 convolution_multiply_fusion
  268.2 0.0 reduce-scatter.5.cloned.1.call-update
  268.2 0.0 reduce-scatter.3.cloned.1.call-start
  268.2 4.0 fusion.8
  272.3 9.3 %broadcast_multiply_fusion = f32[32,1024,64]{1,0,2:T(8,128)} fusion(f32[24,64,1024]{2,1,0:T(8,128)S(1)} %fusion.8, s32[24]{0:T(128)S(1)} %get-tuple-element.12), kind=kOutput, calls=%fused_computation.8 | convolution fusion | flops 606077696 | bytes 14680160 | tf_op jit(solution)/shard_map/ba,bdr->adr/dot_general | solution.py:86
  281.6 0.0 copy-start.3
  281.6 0.0 reduce-scatter.3.cloned.1.call-update
  281.6 0.2 all-gather.3.cloned.1.call-start
  281.8 0.4 all-gather.3.cloned.1.call-update
  282.2 0.5 copy-done.3
  282.7 6.5 %convolution_convert_fusion = bf16[24,128,1024]{2,1,0:T(8,128)(2,1)} fusion(bf16[24,1024,64]{1,2,0:T(8,128)(2,1)} %gather_fusion, f32[24,128,64]{1,2,0:T(8,128)S(1)} %copy-done.3, f32[24,128]{1,0:T(8,128)S(1)} %fusion.9), kind=kOutput, calls=%fused_computation.9 | convolution fusion | flops 406192128 | bytes 10235904 | tf_op jit(solution)/shard_map/qjz,qaz->qja/dot_general | solution.py:66
  289.2 0.0 copy-start.2
  289.2 4.9 all-to-all-start.3
  294.1 0.0 copy-done.2
  294.1 1.3 convolution_convert_fusion.1
  295.4 0.0 reduce-scatter.5.cloned.1.call-done
  295.4 1.7 copy.22
  297.1 225.5 %all-to-all-done.3 = bf16[8,384,1024]{2,1,0:T(8,128)(2,1)} async-done(((bf16[8,384,1024]{2,1,0:T(8,128)(2,1)}), bf16[8,384,1024]{2,1,0:T(8,128)(2,1)}, u32[]{:S(2)}, u32[]{:S(2)}) %all-to-all-start.3) | async-done | bytes 6291488 | tf_op jit(solution)/shard_map/all_to_all | solution.py:77
  522.6 3.5 all-to-all-start.1
  526.2 9.1 %multiply_bitcast_fusion = f32[8,48,8,1024]{3,2,1,0:T(8,128)} fusion(bf16[8,384,1024]{2,1,0:T(8,128)(2,1)} %all-to-all-done.3), kind=kLoop, calls=%fused_computation.3 | loop fusion | flops 6291456 | bytes 18874368
  535.3 11.8 %copy.28 = f32[8,48,8,1024]{3,2,0,1:T(8,128)} copy(f32[8,48,8,1024]{3,2,1,0:T(8,128)} %multiply_bitcast_fusion) | data formatting | bytes 25165824 | tf_op jit(solution)/shard_map/mul | solution.py:96
  547.1 0.0 reduce-scatter.3.cloned.1.call-done
  547.1 4.1 copy.21
  551.2 35.3 %all-gather.3.cloned.1.call-done = bf16[8192,1024]{1,0:T(8,128)(2,1)} async-done(((bf16[1024,1024]{1,0:T(8,128)(2,1)}), bf16[8192,1024]{1,0:T(8,128)(2,1)}) %all-gather.3.cloned.1.call-update) | async-done | bytes 16777232 | tf_op jit(solution)/shard_map/all_gather | solution.py:22
  586.5 14.5 %add_convert_fusion = bf16[384,8192]{1,0:T(8,128)(2,1)} fusion(f32[384,8192]{1,0:T(8,128)} %bitcast.57, bf16[384,1024]{1,0:T(8,128)(2,1)S(1)} %copy-done, bf16[8192,1024]{1,0:T(8,128)(2,1)} %all-gather.3.cloned.1.call-done), kind=kOutput, calls=%fused_computation.2 | convolution fusion | flops 6448742400 | bytes 36438016 | tf_op jit(solution)/shard_map/dot_general | solution.py:24
  601.0 0.0 all-to-all-done.1
  601.0 0.0 copy-start.1
  601.0 12.8 %fusion.5 = bf16[384,1024]{1,0:T(8,128)(2,1)} fusion(bf16[384,8192]{1,0:T(8,128)(2,1)} %param.7, bf16[8192,1024]{1,0:T(8,128)(2,1)} %all-gather.3.cloned.1.call-done, bf16[8,384,128]{2,1,0:T(8,128)(2,1)S(1)} %all-to-all-done.1), kind=kOutput, calls=%fused_computation.11 | convolution fusion | flops 6444023808 | bytes 24641536 | tf_op jit(solution)/shard_map/dot_general | solution.py:23
  613.9 0.0 copy-done.1
  (4 shorter events, 0.0 us)
Async XLA Ops:
  7.2 1.1 copy-start
  9.3 27.3 %all-to-all-start.2 = ((bf16[384,8,128]{2,0,1:T(8,128)(2,1)}), bf16[384,8,128]{2,0,1:T(8,128)(2,1)S(1)}, u32[]{:S(2)}, u32[]{:S(2)}) async-start(bf16[384,8,128]{2,0,1:T(8,128)(2,1)} %copy_bitcast_fusion.1), calls=%async_computation.2 | async-start | bytes 1572864 | tf_op jit(solution)/shard_map/all_to_all | solution.py:44
  36.6 5.7 copy-start.7
  36.6 7.0 %copy-start.5 = (s32[3]{0:T(128)S(1)}, s32[3]{0:T(128)}, u32[]{:S(2)}) copy-start(s32[3]{0:T(128)} %param.12) | copy-start | bytes 40
  36.6 7.2 %copy-start.6 = (s32[3]{0:T(128)S(1)}, s32[3]{0:T(128)}, u32[]{:S(2)}) copy-start(s32[3]{0:T(128)} %param.13) | copy-start | bytes 40
  36.6 144.0 %copy-start.4 = (bf16[8,64,128]{2,1,0:T(8,128)(2,1)S(1)}, bf16[8,64,128]{2,1,0:T(8,128)(2,1)}, u32[]{:S(2)}) copy-start(bf16[8,64,128]{2,1,0:T(8,128)(2,1)} %param.10) | copy-start | bytes 393220
  36.6 160.9 %all-to-all-start = ((bf16[384,8,1024]{2,0,1:T(8,128)(2,1)}), bf16[384,8,1024]{2,0,1:T(8,128)(2,1)}, u32[]{:S(2)}, u32[]{:S(2)}) async-start(bf16[384,8,1024]{2,0,1:T(8,128)(2,1)} %bitcast.55), calls=%async_computation | async-start | bytes 12582912 | tf_op jit(solution)/shard_map/all_to_all | solution.py:43
  41.5 151.3 %all-gather.5.cloned.1.call-start = ((), (), s32[]{:S(2)}) async-start(), calls=%async_computation.7 | async-start | bytes 5242880 | tf_op jit(solution)/shard_map/all_gather | solution.py:28
  42.3 222.3 %all-reduce.6.cloned.1.call-start = ((), (), s32[]{:S(2)}) async-start(), calls=%async_computation.10 | async-start | bytes 3145728 | tf_op jit(solution)/shard_map/psum | solution.py:55
  204.4 91.0 %reduce-scatter.5.cloned.1.call-start = ((), (), s32[]{:S(2)}) async-start(), calls=%async_computation.9 | async-start | bytes 1310720 | tf_op jit(solution)/shard_map/reduce_scatter | solution.py:91
  268.2 278.9 %reduce-scatter.3.cloned.1.call-start = ((), (), s32[]{:S(2)}) async-start(), calls=%async_computation.8 | async-start | bytes 10485760 | tf_op jit(solution)/shard_map/reduce_scatter | solution.py:90
  281.6 1.1 copy-start.3
  281.6 305.0 %all-gather.3.cloned.1.call-start = ((), (), s32[]{:S(2)}) async-start(), calls=%async_computation.6 | async-start | bytes 18874368 | tf_op jit(solution)/shard_map/all_gather | solution.py:22
  289.2 4.9 copy-start.2
  289.2 233.4 %all-to-all-start.3 = ((bf16[8,384,1024]{2,1,0:T(8,128)(2,1)}), bf16[8,384,1024]{2,1,0:T(8,128)(2,1)}, u32[]{:S(2)}, u32[]{:S(2)}) async-start(bf16[8,384,1024]{2,1,0:T(8,128)(2,1)} %bitcast.56), calls=%async_computation.3 | async-start | bytes 12582912 | tf_op jit(solution)/shard_map/all_to_all | solution.py:77
  522.6 78.4 %all-to-all-start.1 = ((bf16[8,384,128]{2,1,0:T(8,128)(2,1)}), bf16[8,384,128]{2,1,0:T(8,128)(2,1)S(1)}, u32[]{:S(2)}, u32[]{:S(2)}) async-start(bf16[8,384,128]{2,1,0:T(8,128)(2,1)} %bitcast.4), calls=%async_computation.1 | async-start | bytes 1572864 | tf_op jit(solution)/shard_map/all_to_all | solution.py:76
  601.0 12.8 %copy-start.1 = (bf16[384,1024]{1,0:T(8,128)(2,1)S(1)}, bf16[384,1024]{1,0:T(8,128)(2,1)}, u32[]{:S(2)}) copy-start(bf16[384,1024]{1,0:T(8,128)(2,1)} %param.11) | copy-start | bytes 2359300
Sparse Core Ops, SparseCore 0:
  44.2 53.9 all-gather.4
  204.5 59.9 all-reduce.5
  268.3 27.0 reduce-scatter.4
  298.4 86.3 reduce-scatter.2
  386.2 200.3 all-gather.2
where the time goes:
time: 621 us; the launch traced here: 620 us
  waiting for transfers between devices  336 us (54%)
  blocking collectives  147 us (24%)
  matrix products  60.4 us (10%)
  local copies, waits for them, and re-layouts  33.2 us (5%)
  starting transfers between devices  20.1 us (3%)
  between operations  14.5 us (2%)
  other arithmetic  9.16 us (1%)
    all_to_all x1, waiting for transfers between devices, body(): lax.all_to_all(spread_input, 'fsdp', split_axis=0, concat_axis=1, tiled=T...  225 us
    unnamed x1, blocking collectives  137 us
    psum x1, waiting for transfers between devices, body(): down_total, up_total = lax.psum((down_partial, up_partial), 'fsdp')  60 us
    all_gather x1, waiting for transfers between devices, body(): piece = lax.all_gather(frozen_value_weight, 'fsdp', axis=0, tiled=True)  35.3 us
    dot_general x1, matrix products, body(): lax.dot_general(output_gradient, piece, (((1,), (1,)), ((), ())), preferr...  14.5 us
    all_to_all x1, waiting for transfers between devices, body(): lax.all_to_all(output_gradient, 'fsdp', split_axis=1, concat_axis=0, tile...  14.4 us
    dot_general x1, matrix products, body(): forward_pass = jnp.dot(tokens, piece, preferred_element_type=jnp.float32)  12.8 us
  transfers between devices with their start and end apart: 9, of which 4 were waited for; matrix products, arithmetic and copies ran while one was open for 12% of the time, Pallas kernels for 0%

commit v1 on v0

v1 whole, which is shorter than its diff:
```python
import jax
import jax.numpy as jnp
from jax import lax
from jax.experimental import pallas as pl
from jax.experimental.pallas import tpu as pltpu
from jax.sharding import PartitionSpec as P

adapter_scale = 0.5
cores = 2


def spread(part, axis):
    size = lax.axis_size(axis)
    copies = jnp.broadcast_to(part[None], (size,) + part.shape)
    return lax.all_to_all(copies, axis, split_axis=0, concat_axis=0, tiled=True)


def gather_frozen(piece, first, second):
    dp, fsdp = lax.axis_size("dp"), lax.axis_size("fsdp")
    rows, width = piece.shape
    chips = fsdp // cores
    share_rows = rows // dp
    share = lax.dynamic_slice_in_dim(piece, lax.axis_index("dp") * share_rows, share_rows, 0)
    same_core = [[chip * cores + core for chip in range(chips)] for core in range(cores)]
    same_chip = [[chip * cores + core for core in range(cores)] for chip in range(chips)]
    shares = lax.all_gather(share, "fsdp", axis=0, axis_index_groups=same_core)
    shares, _ = lax.optimization_barrier((shares, first))
    half = lax.all_gather(shares, "dp", axis=0)
    half, _ = lax.optimization_barrier((half, second))
    return lax.all_gather(half, "fsdp", axis=0, axis_index_groups=same_chip)


def dot(left, right, left_dim, right_dim):
    return lax.dot_general(
        left, right, (((left_dim,), (right_dim,)), ((), ())), preferred_element_type=jnp.float32
    )


def low_rank_kernel(fill_ref, x_ref, dy_ref, pieces_ref, terms_ref, u_ref, v_ref, u_sum, v_sum):
    slices, per_dev, rank, _ = pieces_ref.shape
    block_rows, outputs = dy_ref.shape[2:]
    features = x_ref.shape[1] // slices
    u_sum[...] = jnp.zeros_like(u_sum)
    v_sum[...] = jnp.zeros_like(v_sum)

    def x_of(block, index):
        columns = pl.ds(pl.multiple_of(index * features, features), features)
        return x_ref[block * block_rows : (block + 1) * block_rows, columns]

    @pl.loop(0, slices)
    def _(index):
        for block in range(per_dev):
            u_sum[block] += dot(x_of(block, index), pieces_ref[index, block, :, :features], 1, 1)
            v_sum[block] += dot(dy_ref[index, block], pieces_ref[index, block, :, features:], 1, 1)

    rows = lax.broadcasted_iota(jnp.int32, (block_rows, rank), 0)
    for block in range(per_dev):
        live = (rows < fill_ref[block]).astype(jnp.float32)
        u_ref[block] = (u_sum[block] * live).astype(jnp.bfloat16)
        v_ref[block] = (v_sum[block] * live).astype(jnp.bfloat16)

    @pl.loop(0, slices)
    def _(index):
        for block in range(per_dev):
            down_term = dot(v_ref[block], x_of(block, index), 0, 0)
            up_term = dot(u_ref[block], dy_ref[index, block], 0, 0)
            terms_ref[index, block, :, :features] = down_term.astype(jnp.bfloat16)
            terms_ref[index, block, :, features:] = up_term.astype(jnp.bfloat16)


def low_rank(fill, x, dy, pieces):
    slices, per_dev, rank, _ = pieces.shape
    block_rows = x.shape[0] // per_dev
    low = jax.ShapeDtypeStruct((per_dev, block_rows, rank), jnp.bfloat16)
    vmem = pl.BlockSpec(memory_space=pltpu.VMEM)
    size = 2 * (x.size + dy.size + 2 * pieces.size)
    return pl.pallas_call(
        low_rank_kernel,
        out_shape=(jax.ShapeDtypeStruct(pieces.shape, jnp.bfloat16), low, low),
        in_specs=[pl.BlockSpec(memory_space=pltpu.SMEM), vmem, vmem, vmem],
        out_specs=(vmem, vmem, vmem),
        scratch_shapes=[pltpu.VMEM(low.shape, jnp.float32)] * 2,
        cost_estimate=pl.CostEstimate(
            flops=8 * x.size * rank, bytes_accessed=size, transcendentals=0
        ),
        name="low_rank",
    )(fill, x, dy, pieces)


def combine_kernel(ids_ref, terms_ref, out_ref, total):
    total[...] = jnp.zeros_like(total)

    @pl.loop(0, terms_ref.shape[0])
    def _(block):
        owner = ids_ref[block]
        total[owner] += terms_ref[block].astype(jnp.float32)

    out_ref[...] = total[...].astype(out_ref.dtype)


def combine(ids, terms, adapters):
    shape = (adapters,) + terms.shape[1:]
    vmem = pl.BlockSpec(memory_space=pltpu.VMEM)
    return pl.pallas_call(
        combine_kernel,
        out_shape=jax.ShapeDtypeStruct(shape, jnp.bfloat16),
        in_specs=[pl.BlockSpec(memory_space=pltpu.SMEM), vmem],
        out_specs=vmem,
        scratch_shapes=[pltpu.VMEM(shape, jnp.float32)],
        name="combine",
    )(ids, terms)


def base_kernel(x_ref, dy_ref, w_ref, pieces_ref, up_ref, u_ref, v_ref, y_ref, dx_ref, total):
    index = pl.program_id(0)
    per_dev, block_rows, _ = u_ref.shape
    features = x_ref.shape[1]
    frozen = w_ref[...].reshape(features, w_ref.shape[-1])
    product = dot(x_ref[...], frozen, 1, 0)

    @pl.when(index == 0)
    def _():
        total[...] = product

    @pl.when(index > 0)
    def _():
        total[...] += product

    base_grad = dot(dy_ref[...], frozen, 1, 1)
    for block in range(per_dev):
        rows = slice(block * block_rows, (block + 1) * block_rows)
        pulled = dot(v_ref[block], pieces_ref[0, block, :, :features], 1, 0)
        pulled = pulled.astype(jnp.bfloat16).astype(jnp.float32)
        dx_ref[rows, :] = (base_grad[rows, :] + adapter_scale * pulled).astype(dx_ref.dtype)

    @pl.when(index == pl.num_programs(0) - 1)
    def _():
        for block in range(per_dev):
            rows = slice(block * block_rows, (block + 1) * block_rows)
            lifted = dot(u_ref[block], up_ref[block], 1, 0)
            lifted = lifted.astype(jnp.bfloat16).astype(jnp.float32)
            y_ref[rows, :] = (total[rows, :] + adapter_scale * lifted).astype(y_ref.dtype)


def base(x, dy, gathered, pieces, up, low_u, low_v):
    slices, per_dev, rank, piece_width = pieces.shape
    count_dev, model_width = x.shape
    width = dy.shape[1]
    features = model_width // slices
    _, dp, _, share_rows, _ = gathered.shape

    def whole(array):
        return pl.BlockSpec(array.shape, lambda index: (0,) * array.ndim)

    tile = pl.BlockSpec((count_dev, features), lambda index: (0, index))
    return pl.pallas_call(
        base_kernel,
        grid=(slices,),
        out_shape=(
            jax.ShapeDtypeStruct(dy.shape, jnp.bfloat16),
            jax.ShapeDtypeStruct(x.shape, jnp.bfloat16),
        ),
        in_specs=[
            tile,
            whole(dy),
            pl.BlockSpec(
                (1, dp, 1, share_rows, width),
                lambda index: (index % cores, 0, index // cores, 0, 0),
            ),
            pl.BlockSpec((1, per_dev, rank, piece_width), lambda index: (index, 0, 0, 0)),
            whole(up),
            whole(low_u),
            whole(low_v),
        ],
        out_specs=(whole(dy), tile),
        scratch_shapes=[pltpu.VMEM(dy.shape, jnp.float32)],
        compiler_params=pltpu.CompilerParams(dimension_semantics=("arbitrary",)),
        cost_estimate=pl.CostEstimate(
            flops=4 * x.size * width,
            bytes_accessed=2 * (2 * x.size + model_width * width),
            transcendentals=0,
        ),
        name="base",
    )(x, dy, gathered, pieces, up, low_u, low_v)


def body(
    tokens,
    frozen_value_weight,
    adapter_down_weight,
    adapter_up_weight,
    output_gradient,
    adapter_per_block,
    block_live_count,
):
    dp, fsdp = lax.axis_size("dp"), lax.axis_size("fsdp")
    count_dev, model_width = tokens.shape
    value_width = output_gradient.shape[1]
    per_dev = adapter_per_block.shape[0]
    block_rows = count_dev // per_dev
    own, features, rank = adapter_down_weight.shape
    outputs = adapter_up_weight.shape[2]
    total = own * dp
    ids_all = lax.all_gather(adapter_per_block, "fsdp", axis=0, tiled=True)
    ids_all, down, up = lax.optimization_barrier(
        (ids_all, adapter_down_weight, adapter_up_weight)
    )
    pieces = jnp.concatenate([down.transpose(0, 2, 1), up], axis=2)
    catalog_pieces = spread(pieces, "dp").reshape(total, rank, features + outputs)
    chosen = catalog_pieces[ids_all].reshape(fsdp, per_dev, rank, features + outputs)
    arrived = lax.all_to_all(chosen, "fsdp", split_axis=0, concat_axis=0, tiled=True)
    up_blocks = arrived[..., features:].transpose(1, 2, 0, 3).reshape(per_dev, rank, value_width)
    dy_slices = output_gradient.reshape(per_dev, block_rows, fsdp, outputs).transpose(2, 0, 1, 3)
    terms, low_u, low_v = low_rank(block_live_count, tokens, dy_slices, arrived)
    terms = lax.all_to_all(terms, "fsdp", split_axis=0, concat_axis=0, tiled=True)
    terms = terms.reshape(fsdp * per_dev, rank, features + outputs)
    sums = combine(ids_all, terms, total).reshape(dp, own, rank, features + outputs)
    sums = lax.all_to_all(sums, "dp", split_axis=0, concat_axis=0, tiled=True)
    gathered = gather_frozen(frozen_value_weight, catalog_pieces, terms)
    values, input_gradient = base(
        tokens, output_gradient, gathered, arrived, up_blocks, low_u, low_v
    )
    sums, values, input_gradient = lax.optimization_barrier((sums, values, input_gradient))
    gradients = adapter_scale * jnp.sum(sums.astype(jnp.float32), axis=0)
    grad_down = gradients[..., :features].transpose(0, 2, 1)
    grad_up = gradients[..., features:]
    return values, input_gradient, grad_down, grad_up


def solution(mesh):
    placed = (
        P(("dp", "fsdp"), None),
        P("fsdp", None),
        P("dp", "fsdp", None),
        P("dp", None, "fsdp"),
        P(("dp", "fsdp"), None),
        P(("dp", "fsdp")),
        P(("dp", "fsdp")),
    )
    return jax.shard_map(
        body,
        mesh=mesh,
        in_specs=placed,
        out_specs=(
            P(("dp", "fsdp"), None),
            P(("dp", "fsdp"), None),
            P("dp", "fsdp", None),
            P("dp", None, "fsdp"),
        ),
        check_vma=False,
    )
```

time: 621 us -> 346 us (0.56)
  waiting for transfers between devices: 336 us -> 158 us
  matrix products: 60.4 us -> 0 us
  blocking collectives: 147 us -> 95 us
  Pallas kernels: 0 us -> 41.2 us
  local copies, waits for them, and re-layouts: 33.2 us -> 16.8 us
    all_to_all x4 -> x3, waiting for transfers between devices: 240 us -> 96.8 us  [the longest x1 78.6 us: body(): lax.all_to_all(chosen, 'fsdp', split_axis=0, concat_axis=0, tiled=True)]
    unnamed x1 -> x0, blocking collectives: 137 us -> none
    all_to_all x0 -> x1, blocking collectives: none -> 84.4 us  [body(): lax.all_to_all(terms, 'fsdp', split_axis=0, concat_axis=0, tiled=True)]
    dot_general x10 -> x0, matrix products: 60.4 us -> none  [the longest x1 14.5 us: body(): lax.dot_general(output_gradient, piece, (((1,), (1,)), ((), ())), preferr...]
    psum x1 -> x0, waiting for transfers between devices: 60 us -> none  [body(): down_total, up_total = lax.psum((down_partial, up_partial), 'fsdp')]
    pallas_call x0 -> x3, Pallas kernels: none -> 41.2 us  [the longest x1 23 us: base(): pl.pallas_call(base_kernel, grid=(slices,), out_shape=(jax.ShapeDtypeStru...]
    all_gather x2 -> x3, waiting for transfers between devices: 35.3 us -> 60.8 us  [the longest x1 46.6 us: gather_frozen(): shares = lax.all_gather(share, 'fsdp', axis=0, axis_index_groups=same_core)]
    mul x1 -> x0, local copies, waits for them, and re-layouts: 11.8 us -> none  [body(): adapter_scale * input_resident.astype(jnp.float32)]
  transfers between devices with their start and end apart: 9 -> 6, of which waited for: 4 -> 5; matrix products, arithmetic and copies ran while one was open for 12% -> 3% of each run, Pallas kernels for 0% -> 12%
where the time goes in v1:
time: 346 us; the launch traced here: 345 us
  waiting for transfers between devices  158 us (46%)
  blocking collectives  95 us (27%)
  Pallas kernels  41.2 us (12%)
  local copies, waits for them, and re-layouts  16.8 us (5%)
  starting transfers between devices  15.1 us (4%)
  between operations  14.5 us (4%)
  other arithmetic  4.98 us (1%)
    all_to_all x1, blocking collectives, body(): lax.all_to_all(terms, 'fsdp', split_axis=0, concat_axis=0, tiled=True)  84.4 us
    all_to_all x1, waiting for transfers between devices, body(): lax.all_to_all(chosen, 'fsdp', split_axis=0, concat_axis=0, tiled=True)  78.6 us
    all_gather x1, waiting for transfers between devices, gather_frozen(): shares = lax.all_gather(share, 'fsdp', axis=0, axis_index_groups=same_core)  46.6 us
    pallas_call x1, Pallas kernels, base(): pl.pallas_call(base_kernel, grid=(slices,), out_shape=(jax.ShapeDtypeStru...  23 us
    all_gather x1, waiting for transfers between devices, gather_frozen(): return lax.all_gather(half, 'fsdp', axis=0, axis_index_groups=same_chip)  14.2 us
    all_to_all x1, waiting for transfers between devices, body(): sums = lax.all_to_all(sums, 'dp', split_axis=0, concat_axis=0, tiled=True)  14 us
    pallas_call x1, Pallas kernels, low_rank(): pl.pallas_call(low_rank_kernel, out_shape=(jax.ShapeDtypeStruct(pieces.sh...  11.4 us
    optimization_barrier x1, blocking collectives, body(): lax.optimization_barrier((ids_all, adapter_down_weight, adapter_up_weight))  10.6 us
  transfers between devices with their start and end apart: 6, of which 5 were waited for; matrix products, arithmetic and copies ran while one was open for 3% of the time, Pallas kernels for 12%

profile of v1, /device:TPU:0, one launch (start us, length us, event | category | flops | bytes accessed | tf_op | source)
XLA Modules:
  0.0 345.2 jit_solution(10289707199115874506)
XLA Ops:
  7.2 0.0 copy-start
  7.2 1.4 dynamic-slice
  9.2 0.9 dynamic-update-slice
  10.1 10.6 %all-reduce.ids_ref = s32[24]{0:T(128)S(1)} all-reduce(s32[24]{0:T(128)S(1)} %dynamic-update-slice), channel_id=1, replica_groups=mesh['dp'=4,'fsdp'=8] {'fsdp'}, use_global_device_ids=true, to_apply=%add | all-reduce | flops 24 | bytes 192 | tf_op jit(solution)/shard_map/optimization_barrier | solution.py:205
  20.7 0.0 copy-start.3
  20.7 1.4 pad_maximum_fusion
  22.2 2.8 broadcast_in_dim.4
  25.0 5.0 %all-to-all-start = ((bf16[4,8,64,1152]{3,2,1,0:T(8,128)(2,1)}), bf16[4,8,64,1152]{3,2,1,0:T(8,128)(2,1)}, u32[]{:S(2)}, u32[]{:S(2)}) async-start(bf16[4,8,64,1152]{3,2,1,0:T(8,128)(2,1)} %broadcast_in_dim.4), calls=%async_computation | async-start | bytes 9437184 | tf_op jit(solution)/shard_map/all_to_all | solution.py:15
  30.0 0.0 all-gather.7.cloned.1.call-start
  30.0 0.0 copy-done
  30.0 0.8 constant_dynamic-slice_fusion
  30.9 0.0 all-gather.7.cloned.1.call-update
  30.9 0.0 all-gather.9.cloned.1.call-start
  31.0 0.0 copy-done.3
  31.0 46.6 %all-gather.7.cloned.1.call-done = bf16[1024,1024]{1,0:T(8,128)(2,1)} async-done(((bf16[256,1024]{1,0:T(8,128)(2,1)}), bf16[1024,1024]{1,0:T(8,128)(2,1)}) %all-gather.7.cloned.1.call-update) | async-done | bytes 2097168 | tf_op jit(solution)/shard_map/all_gather | solution.py:26
  77.5 4.2 %all-to-all-done = bf16[4,8,64,1152]{3,2,1,0:T(8,128)(2,1)} async-done(((bf16[4,8,64,1152]{3,2,1,0:T(8,128)(2,1)}), bf16[4,8,64,1152]{3,2,1,0:T(8,128)(2,1)}, u32[]{:S(2)}, u32[]{:S(2)}) %all-to-all-start) | async-done | bytes 4718624 | tf_op jit(solution)/shard_map/all_to_all | solution.py:15
  81.7 0.0 all-gather.9.cloned.1.call-update
  81.8 5.4 %gather_fusion = bf16[24,64,1152]{2,1,0:T(8,128)(2,1)} fusion(bf16[32,64,1152]{2,1,0:T(8,128)(2,1)} %bitcast.3, s32[1024]{0:T(1024)S(1)} %pad_clamp_fusion), kind=kCustom, calls=%fused_computation | custom fusion | bytes 7077984 | tf_op jit(solution)/shard_map/gather | solution.py:210
  87.2 0.0 copy-start.2
  87.2 4.8 %all-to-all-start.1 = ((bf16[8,3,64,1152]{3,2,1,0:T(8,128)(2,1)}), bf16[8,3,64,1152]{3,2,1,0:T(8,128)(2,1)}, u32[]{:S(2)}, u32[]{:S(2)}) async-start(bf16[8,3,64,1152]{3,2,1,0:T(8,128)(2,1)} %bitcast.24), calls=%async_computation.1 | async-start | bytes 7077888 | tf_op jit(solution)/shard_map/all_to_all | solution.py:211
  91.9 0.0 all-gather.11.cloned.1.call-start
  92.0 0.0 copy-done.2
  92.0 0.2 copy.17
  92.2 1.1 copy.20
  93.2 78.6 %all-to-all-done.1.pieces_ref = bf16[8,3,64,1152]{3,2,1,0:T(8,128)(2,1)} async-done(((bf16[8,3,64,1152]{3,2,1,0:T(8,128)(2,1)}), bf16[8,3,64,1152]{3,2,1,0:T(8,128)(2,1)}, u32[]{:S(2)}, u32[]{:S(2)}) %all-to-all-start.1) | async-done | bytes 3538976 | tf_op jit(solution)/shard_map/all_to_all | solution.py:211
  171.9 11.4 %low_rank.1 = (bf16[8,3,64,1152]{3,2,1,0:T(8,128)(2,1)}, bf16[3,128,64]{2,1,0:T(8,128)(2,1)}, bf16[3,128,64]{2,1,0:T(8,128)(2,1)}) custom-call(s32[3]{0:T(128)} %fill_ref.1, bf16[384,8192]{1,0:T(8,128)(2,1)} %x_ref.3, bf16[8,3,128,128]{3,2,1,0:T(8,128)(2,1)} %bitcast.28, bf16[8,3,64,1152]{3,2,1,0:T(8,128)(2,1)} %all-to-all-done.1.pieces_ref), custom_call_target="tpu_custom_call" | custom-call | flops 1610612736 | bytes 14155776 | tf_op jit(solution)/shard_map/low_rank/pallas_call | solution.py:77
  183.3 84.4 %all_to_all.20 = bf16[8,3,64,1152]{3,2,1,0:T(8,128)(2,1)} all-to-all(bf16[8,3,64,1152]{3,2,1,0:T(8,128)(2,1)} %get-tuple-element.20), channel_id=1, replica_groups=mesh['dp'=4,'fsdp'=8] {'fsdp'}, dimensions={0} | all-to-all | bytes 7077888 | tf_op jit(solution)/shard_map/all_to_all | solution.py:215
  267.7 0.0 all-gather.9.cloned.1.call-done
  267.7 0.0 all-gather.11.cloned.1.call-update
  267.7 6.7 %combine.1 = bf16[32,64,1152]{2,1,0:T(8,128)(2,1)} custom-call(s32[24]{0:T(128)} %copy-done.3, bf16[24,64,1152]{2,1,0:T(8,128)(2,1)} %bitcast.25), custom_call_target="tpu_custom_call" | custom-call | tf_op jit(solution)/shard_map/combine/pallas_call | solution.py:104
  274.4 5.3 %all-to-all-start.3 = ((bf16[4,8,64,1152]{3,2,1,0:T(8,128)(2,1)}), bf16[4,8,64,1152]{3,2,1,0:T(8,128)(2,1)}, u32[]{:S(2)}, u32[]{:S(2)}) async-start(bf16[4,8,64,1152]{3,2,1,0:T(8,128)(2,1)} %bitcast.23), calls=%async_computation.3 | async-start | bytes 9437184 | tf_op jit(solution)/shard_map/all_to_all | solution.py:218
  279.7 1.9 copy_bitcast_fusion.1.up_ref
  281.6 14.2 %all-gather.11.cloned.1.call-done = bf16[8,4,256,1024]{3,2,1,0:T(8,128)(2,1)} async-done(((bf16[4,4,256,1024]{3,2,1,0:T(8,128)(2,1)}), bf16[8,4,256,1024]{3,2,1,0:T(8,128)(2,1)}) %all-gather.11.cloned.1.call-update) | async-done | bytes 16777232 | tf_op jit(solution)/shard_map/all_gather | solution.py:30
  295.8 23.0 %base.1 = (bf16[384,1024]{1,0:T(8,128)(2,1)}, bf16[384,8192]{1,0:T(8,128)(2,1)}) custom-call(bf16[384,8192]{1,0:T(8,128)(2,1)} %x_ref.3, bf16[384,1024]{1,0:T(8,128)(2,1)} %dy_ref.1, bf16[2,4,4,256,1024]{4,3,2,1,0:T(8,128)(2,1)} %bitcast.32, bf16[8,3,64,1152]{3,2,1,0:T(8,128)(2,1)} %all-to-all-done.1.pieces_ref, ...), custom_call_target="tpu_custom_call" | custom-call | flops 12884901888 | bytes 29360128 | tf_op jit(solution)/shard_map/base/pallas_call | solution.py:156
  318.8 14.0 %all-to-all-done.3 = bf16[4,8,64,1152]{3,2,1,0:T(8,128)(2,1)} async-done(((bf16[4,8,64,1152]{3,2,1,0:T(8,128)(2,1)}), bf16[4,8,64,1152]{3,2,1,0:T(8,128)(2,1)}, u32[]{:S(2)}, u32[]{:S(2)}) %all-to-all-start.3) | async-done | bytes 4718624 | tf_op jit(solution)/shard_map/all_to_all | solution.py:218
  332.8 3.4 convert_reduce_fusion
  336.1 0.0 copy-start.1
  336.2 0.2 broadcast_multiply_fusion
  336.3 1.6 slice_bitcast_fusion
  338.0 0.7 slice.16
  338.7 0.0 copy-done.1
  (3 shorter events, 0.0 us)
Async XLA Ops:
  7.2 22.9 %copy-start = (bf16[1024,1024]{1,0:T(8,128)(2,1)S(1)}, bf16[1024,1024]{1,0:T(8,128)(2,1)}, u32[]{:S(2)}) copy-start(bf16[1024,1024]{1,0:T(8,128)(2,1)} %param.8) | copy-start | bytes 6291460
  20.7 10.2 %copy-start.3 = (s32[24]{0:T(128)}, s32[24]{0:T(128)S(1)}, u32[]{:S(2)}) copy-start(s32[24]{0:T(128)S(1)} %all-reduce.ids_ref) | copy-start | bytes 292
  25.0 56.7 %all-to-all-start = ((bf16[4,8,64,1152]{3,2,1,0:T(8,128)(2,1)}), bf16[4,8,64,1152]{3,2,1,0:T(8,128)(2,1)}, u32[]{:S(2)}, u32[]{:S(2)}) async-start(bf16[4,8,64,1152]{3,2,1,0:T(8,128)(2,1)} %broadcast_in_dim.4), calls=%async_computation | async-start | bytes 9437184 | tf_op jit(solution)/shard_map/all_to_all | solution.py:15
  30.0 47.6 %all-gather.7.cloned.1.call-start = ((), (), s32[]{:S(2)}) async-start(), calls=%async_computation.4 | async-start | bytes 2621440 | tf_op jit(solution)/shard_map/all_gather | solution.py:26
  30.9 236.8 %all-gather.9.cloned.1.call-start = ((), (), s32[]{:S(2)}) async-start(), calls=%async_computation.5 | async-start | bytes 10485760 | tf_op jit(solution)/shard_map/all_gather | solution.py:28
  87.2 4.8 %copy-start.2 = (bf16[384,1024]{1,0:T(8,128)(2,1)S(1)}, bf16[384,1024]{1,0:T(8,128)(2,1)}, u32[]{:S(2)}) copy-start(bf16[384,1024]{1,0:T(8,128)(2,1)} %dy_ref.1) | copy-start | bytes 2359300
  87.2 84.7 %all-to-all-start.1 = ((bf16[8,3,64,1152]{3,2,1,0:T(8,128)(2,1)}), bf16[8,3,64,1152]{3,2,1,0:T(8,128)(2,1)}, u32[]{:S(2)}, u32[]{:S(2)}) async-start(bf16[8,3,64,1152]{3,2,1,0:T(8,128)(2,1)} %bitcast.24), calls=%async_computation.1 | async-start | bytes 7077888 | tf_op jit(solution)/shard_map/all_to_all | solution.py:211
  91.9 203.9 %all-gather.11.cloned.1.call-start = ((), (), s32[]{:S(2)}) async-start(), calls=%async_computation.6 | async-start | bytes 25165824 | tf_op jit(solution)/shard_map/all_gather | solution.py:30
  274.4 58.4 %all-to-all-start.3 = ((bf16[4,8,64,1152]{3,2,1,0:T(8,128)(2,1)}), bf16[4,8,64,1152]{3,2,1,0:T(8,128)(2,1)}, u32[]{:S(2)}, u32[]{:S(2)}) async-start(bf16[4,8,64,1152]{3,2,1,0:T(8,128)(2,1)} %bitcast.23), calls=%async_computation.3 | async-start | bytes 9437184 | tf_op jit(solution)/shard_map/all_to_all | solution.py:218
  336.1 2.5 copy-start.1
Sparse Core Ops, SparseCore 0:
  32.9 44.5 all-gather.6
  81.9 84.7 all-gather.8
  267.8 27.9 all-gather.10
